TPU v7x, 32 devices: a whole 2x2x4 slice. The times are simulated.
32 devices in a mesh: grp: 4 (over z), grid: 8 (over y, x, core).
Axes of the slice: x: 2, y: 2, z: 4, core: 2. Of those that a mesh axis runs over, the one named last changes fastest.
Arguments:
- vectors: float32 [4, 3, 2, 32, 256, 256], P('grp', None, None, 'grid'), may hold values from -6 to 6
- potential: float32 [32, 256, 256], P('grid'), may hold values from 0.1 to 2
- added_field: float32 [4, 32, 256, 256], P('grp', 'grid'), may hold values from -3 to 3
- qp_states: bfloat16 [32, 32, 256, 256], P(None, 'grid'), may hold values from -0.00390625 to 0.00390625
Outputs:
- elements: float32 [4, 32, 6], P('grp', 'grid')
All inputs are finite; a program needn't handle non-finite values.
Results may differ from a plain program's by a relative error of at most 0.0033.
Values sent between devices are 32-bit elements; how exact they have to be, the bound alone decides.
No kernel may reach another device: no remote copies, remote signals or barrier semaphores. Data moves between devices by JAX's collectives and lax.ppermute only.
A program may use at most 256 MiB of HBM per device.

v0:
```python
import jax
import jax.numpy as jnp
from jax import lax
from jax.sharding import PartitionSpec as P

ORDER = 4
time_step = 0.2
four_pi = 12.566370614359172


def padded_2(block, sides, width):
    for axis, dim in sides:
        count = lax.axis_size(axis)
        forward = [(i, i + 1) for i in range(count - 1)]
        backward = [(target, source) for source, target in forward]
        low = lax.ppermute(
            lax.slice_in_dim(block, block.shape[dim] - width, None, axis=dim), axis, forward
        )
        high = lax.ppermute(lax.slice_in_dim(block, 0, width, axis=dim), axis, backward)
        block = jnp.concatenate([low, block, high], axis=dim)
    return block


def shifted(array, axis, by):
    peers = lax.axis_size(axis)
    pairs = [(i, i + by) for i in range(peers) if 0 <= i + by < peers]
    return lax.ppermute(array, axis, pairs)


def sine_table(length):
    indices = jnp.arange(length, dtype=jnp.int32) + 1
    products = indices[:, None] * indices[None, :] % (2 * (length + 1))
    return jnp.sqrt(2.0 / (length + 1)) * jnp.sin(
        jnp.pi * products.astype(jnp.float32) / (length + 1)
    )


def eigenvalues(length):
    indices = jnp.arange(length, dtype=jnp.int32) + 1
    return 2.0 - 2.0 * jnp.cos(jnp.pi * indices.astype(jnp.float32) / (length + 1))


def laplace_inner(field):
    centre = field[..., 1:-1, :, :]
    result = field[..., 2:, :, :] + field[..., :-2, :, :]
    widths = [(0, 0)] * (centre.ndim - 2)
    along_y = jnp.pad(centre, widths + [(1, 1), (0, 0)])
    result = result + along_y[..., 2:, :] + along_y[..., :-2, :]
    along_z = jnp.pad(centre, widths + [(0, 0), (1, 1)])
    result = result + along_z[..., 2:] + along_z[..., :-2]
    return result - 6.0 * centre


def taylor_term(applied, power):
    factor = time_step / power
    return jnp.stack([factor * applied[:, :, 1], -factor * applied[:, :, 0]], axis=2)


def poisson_block(density):
    highest = lax.Precision.HIGHEST
    planes = density.shape[0]
    size_y = density.shape[1]
    size_z = density.shape[2]
    full_x = planes * lax.axis_size("grid")
    table_x = sine_table(full_x)
    table_y = sine_table(size_y)
    table_z = sine_table(size_z)
    field = jnp.einsum("xyz,zl->xyl", density, table_z, precision=highest)
    field = jnp.einsum("xyl,yk->xkl", field, table_y, precision=highest)
    columns = lax.all_to_all(field, "grid", split_axis=1, concat_axis=0, tiled=True)
    row_count = columns.shape[1]
    own_rows = lax.dynamic_slice_in_dim(
        eigenvalues(size_y), lax.axis_index("grid") * row_count, row_count
    )
    field = jnp.einsum("xkl,xm->mkl", columns, table_x, precision=highest)
    spectrum = (
        eigenvalues(full_x)[:, None, None]
        + own_rows[None, :, None]
        + eigenvalues(size_z)[None, None, :]
    )
    field = field * (four_pi / spectrum)
    field = jnp.einsum("mkl,mx->xkl", field, table_x, precision=highest)
    returned = lax.all_to_all(field, "grid", split_axis=0, concat_axis=1, tiled=True)
    field = jnp.einsum("xkl,ky->xyl", returned, table_y, precision=highest)
    return jnp.einsum("xyl,lz->xyz", field, table_z, precision=highest)


def on_device(vectors, potential, added_field, qp_states):
    initial = vectors[0]
    state = jnp.stack([initial, initial])
    fields = jnp.stack([potential, potential + added_field[0]])
    summed = state
    current = state
    for power in range(1, ORDER + 1):
        padded = padded_2(current, (("grid", 3),), 1)
        applied = -0.5 * laplace_inner(padded) + fields[:, None, None] * current
        current = taylor_term(applied, power)
        summed = summed + current
    density = jnp.sum(summed[1] * summed[1] - summed[0] * summed[0], axis=(0, 1))
    induced = poisson_block(density)
    received = shifted(induced, "grp", lax.axis_size("grp") // 2)
    weighted = ((received + added_field[0]) * summed[1]).astype(jnp.bfloat16)
    flat_weighted = weighted.reshape(weighted.shape[0] * weighted.shape[1], -1)
    flat_states = qp_states.reshape(qp_states.shape[0], -1)
    result = lax.psum_scatter(
        jnp.dot(flat_states, flat_weighted.T, preferred_element_type=jnp.float32),
        "grid",
        scatter_dimension=0,
        tiled=True,
    )
    return result[None]


def solution(mesh):
    in_specs = (
        P("grp", None, None, "grid", None, None),
        P("grid", None, None),
        P("grp", "grid", None, None),
        P(None, "grid", None, None),
    )
    out_specs = P("grp", "grid", None)
    return jax.shard_map(
        on_device, mesh=mesh, in_specs=in_specs, out_specs=out_specs, check_vma=False
    )
```

profile of v0, /device:TPU:28, one launch (start us, length us, event | category | flops | bytes accessed | tf_op | source)
XLA Modules:
  0.0 656.1 jit_solution(16886512140315843217)
XLA Ops:
  0.0 3.6 constant_dynamic-update-slice_fusion.1
  5.7 4.5 copy-done.4
  10.8 2.8 collective-permute-start
  13.6 1.9 collective-permute-start.1
  15.9 64.2 %collective-permute-done = f32[2,3,2,1,256,256]{5,4,3,2,1,0:T(8,128)} collective-permute-done((f32[2,3,2,1,256,256]{5,4,3,2,1,0:T(8,128)S(1)}, f32[2,3,2,1,256,256]{5,4,3,2,1,0:T(8,128)}, u32[]{:S(2)}, u32[]{:S(2)}) %collective-permute-start) | collective-permute-done | bytes 3145760 | tf_op jit(solution)/shard_map/ppermute | solution.py:19
  80.1 3.1 collective-permute-done.1
  83.2 33.2 %fusion.4 = f32[2,3,2,4,256,256]{5,4,3,2,1,0:T(8,128)} fusion(f32[2,3,2,4,256,256]{5,4,3,2,1,0:T(8,128)} %copy-done.4, f32[2,3,2,1,256,256]{5,4,3,2,1,0:T(8,128)} %collective-permute-done.1, f32[2,3,2,1,256,256]{5,4,3,2,1,0:T(8,128)} %collective-permute-done, f32[2,4,256,256]{3,2,1,0:T(8,128)S(1)} %pad_maximum_fusion.17), kind=kLoop, calls=%fused_computation.27 | loop fusion | flops 37748736 | bytes 33554432 | tf_op jit(solution)/shard_map/add | solution.py:96
  116.4 8.8 %slice_multiply_fusion.8 = (f32[2,3,1,4,256,256]{5,4,3,2,1,0:T(8,128)S(1)}, f32[2,3,1,4,256,256]{5,4,3,2,1,0:T(8,128)}) fusion(f32[2,3,2,4,256,256]{5,4,3,2,1,0:T(8,128)} %fusion.4), kind=kLoop, calls=%fused_computation.80 | loop fusion | flops 3145728 | bytes 25165824 | tf_op jit(solution)/shard_map/mul | solution.py:56
  125.1 7.3 %fusion.38 = (f32[2,3,2,1,256,256]{5,4,3,2,1,0:T(8,128)}, f32[2,3,2,1,256,256]{5,4,3,2,1,0:T(8,128)}) fusion(f32[2,3,1,4,256,256]{5,4,3,2,1,0:T(8,128)S(1)} %get-tuple-element.17, f32[2,3,1,4,256,256]{5,4,3,2,1,0:T(8,128)} %get-tuple-element.18), kind=kLoop, calls=%fused_computation.86 | loop fusion | flops 1572864 | bytes 18874368 | tf_op jit(solution)/shard_map/stack | solution.py:56
  132.5 1.9 collective-permute-start.2
  134.4 2.4 collective-permute-start.3
  136.8 8.7 %pad_maximum_fusion = f32[2,3,2,4,256,256]{5,4,3,2,1,0:T(8,128)} fusion(f32[2,3,1,4,256,256]{5,4,3,2,1,0:T(8,128)} %get-tuple-element.18, f32[2,3,1,4,256,256]{5,4,3,2,1,0:T(8,128)S(1)} %get-tuple-element.17), kind=kLoop, calls=%fused_computation.10 | loop fusion | flops 3145728 | bytes 25165824 | tf_op jit(solution)/shard_map/stack | solution.py:56
  145.5 54.8 %collective-permute-done.2 = f32[2,3,2,1,256,256]{5,4,3,2,1,0:T(8,128)} collective-permute-done((f32[2,3,2,1,256,256]{5,4,3,2,1,0:T(8,128)}, f32[2,3,2,1,256,256]{5,4,3,2,1,0:T(8,128)}, u32[]{:S(2)}, u32[]{:S(2)}) %collective-permute-start.2) | collective-permute-done | bytes 3145760 | tf_op jit(solution)/shard_map/ppermute | solution.py:19
  201.4 34.5 %fusion.9 = f32[2,3,2,4,256,256]{5,4,3,2,1,0:T(8,128)} fusion(f32[2,3,2,4,256,256]{5,4,3,2,1,0:T(8,128)} %pad_maximum_fusion, f32[2,3,2,1,256,256]{5,4,3,2,1,0:T(8,128)} %collective-permute-done.3, f32[2,3,1,4,256,256]{5,4,3,2,1,0:T(8,128)} %get-tuple-element.18, f32[2,3,1,4,256,256]{5,4,3,2,1,0:T(8,128)} %copy-done, ...), kind=kLoop, calls=%fused_computation.32 | loop fusion | flops 44040192 | bytes 46137344 | tf_op jit(solution)/shard_map/add | solution.py:96
  235.8 8.8 %slice_multiply_fusion.6 = (f32[2,3,1,4,256,256]{5,4,3,2,1,0:T(8,128)S(1)}, f32[2,3,1,4,256,256]{5,4,3,2,1,0:T(8,128)}) fusion(f32[2,3,2,4,256,256]{5,4,3,2,1,0:T(8,128)} %fusion.9), kind=kLoop, calls=%fused_computation.78 | loop fusion | flops 3145728 | bytes 25165824 | tf_op jit(solution)/shard_map/mul | solution.py:56
  244.6 7.5 %fusion.36 = (f32[2,3,2,1,256,256]{5,4,3,2,1,0:T(8,128)}, f32[2,3,2,1,256,256]{5,4,3,2,1,0:T(8,128)}) fusion(f32[2,3,1,4,256,256]{5,4,3,2,1,0:T(8,128)S(1)} %get-tuple-element.13, f32[2,3,1,4,256,256]{5,4,3,2,1,0:T(8,128)} %get-tuple-element.14), kind=kLoop, calls=%fused_computation.84 | loop fusion | flops 1572864 | bytes 18874368 | tf_op jit(solution)/shard_map/stack | solution.py:56
  252.1 3.7 collective-permute-start.4
  255.8 2.2 collective-permute-start.5
  258.0 8.8 %pad_maximum_fusion.1 = f32[2,3,2,4,256,256]{5,4,3,2,1,0:T(8,128)} fusion(f32[2,3,1,4,256,256]{5,4,3,2,1,0:T(8,128)} %get-tuple-element.14, f32[2,3,1,4,256,256]{5,4,3,2,1,0:T(8,128)S(1)} %get-tuple-element.13), kind=kLoop, calls=%fused_computation.15 | loop fusion | flops 3145728 | bytes 25165824 | tf_op jit(solution)/shard_map/stack | solution.py:56
  266.8 53.9 %collective-permute-done.4 = f32[2,3,2,1,256,256]{5,4,3,2,1,0:T(8,128)} collective-permute-done((f32[2,3,2,1,256,256]{5,4,3,2,1,0:T(8,128)}, f32[2,3,2,1,256,256]{5,4,3,2,1,0:T(8,128)}, u32[]{:S(2)}, u32[]{:S(2)}) %collective-permute-start.4) | collective-permute-done | bytes 3145760 | tf_op jit(solution)/shard_map/ppermute | solution.py:19
  320.8 34.4 %fusion.14 = f32[2,3,2,4,256,256]{5,4,3,2,1,0:T(8,128)} fusion(f32[2,3,2,4,256,256]{5,4,3,2,1,0:T(8,128)} %pad_maximum_fusion.1, f32[2,3,2,1,256,256]{5,4,3,2,1,0:T(8,128)} %collective-permute-done.5, f32[2,3,1,4,256,256]{5,4,3,2,1,0:T(8,128)} %get-tuple-element.14, f32[2,3,1,4,256,256]{5,4,3,2,1,0:T(8,128)} %copy-done.1, ...), kind=kLoop, calls=%fused_computation.37 | loop fusion | flops 44040192 | bytes 46137344 | tf_op jit(solution)/shard_map/add | solution.py:96
  355.2 8.7 %slice_multiply_fusion.4 = (f32[2,3,1,4,256,256]{5,4,3,2,1,0:T(8,128)S(1)}, f32[2,3,1,4,256,256]{5,4,3,2,1,0:T(8,128)}) fusion(f32[2,3,2,4,256,256]{5,4,3,2,1,0:T(8,128)} %fusion.14), kind=kLoop, calls=%fused_computation.76 | loop fusion | flops 3145728 | bytes 25165824 | tf_op jit(solution)/shard_map/mul | solution.py:56
  363.9 7.4 %fusion.34 = (f32[2,3,2,1,256,256]{5,4,3,2,1,0:T(8,128)}, f32[2,3,2,1,256,256]{5,4,3,2,1,0:T(8,128)}) fusion(f32[2,3,1,4,256,256]{5,4,3,2,1,0:T(8,128)S(1)} %get-tuple-element.9, f32[2,3,1,4,256,256]{5,4,3,2,1,0:T(8,128)} %get-tuple-element.10), kind=kLoop, calls=%fused_computation.82 | loop fusion | flops 1572864 | bytes 18874368 | tf_op jit(solution)/shard_map/stack | solution.py:56
  371.3 4.7 collective-permute-start.6
  376.1 3.1 collective-permute-start.7
  379.1 8.8 %pad_maximum_fusion.2 = f32[2,3,2,4,256,256]{5,4,3,2,1,0:T(8,128)} fusion(f32[2,3,1,4,256,256]{5,4,3,2,1,0:T(8,128)} %get-tuple-element.10, f32[2,3,1,4,256,256]{5,4,3,2,1,0:T(8,128)S(1)} %get-tuple-element.9), kind=kLoop, calls=%fused_computation.20 | loop fusion | flops 3145728 | bytes 25165824 | tf_op jit(solution)/shard_map/stack | solution.py:56
  387.9 52.1 %collective-permute-done.6 = f32[2,3,2,1,256,256]{5,4,3,2,1,0:T(8,128)} collective-permute-done((f32[2,3,2,1,256,256]{5,4,3,2,1,0:T(8,128)}, f32[2,3,2,1,256,256]{5,4,3,2,1,0:T(8,128)}, u32[]{:S(2)}, u32[]{:S(2)}) %collective-permute-start.6) | collective-permute-done | bytes 3145760 | tf_op jit(solution)/shard_map/ppermute | solution.py:19
  440.0 34.5 %fusion.19 = f32[2,3,2,4,256,256]{5,4,3,2,1,0:T(8,128)} fusion(f32[2,3,2,4,256,256]{5,4,3,2,1,0:T(8,128)} %pad_maximum_fusion.2, f32[2,3,2,1,256,256]{5,4,3,2,1,0:T(8,128)} %collective-permute-done.7, f32[2,3,1,4,256,256]{5,4,3,2,1,0:T(8,128)} %get-tuple-element.10, f32[2,3,1,4,256,256]{5,4,3,2,1,0:T(8,128)} %copy-done.2, ...), kind=kLoop, calls=%fused_computation.42 | loop fusion | flops 44040192 | bytes 46137344 | tf_op jit(solution)/shard_map/add | solution.py:96
  474.5 11.2 %slice_multiply_fusion.2 = (f32[2,3,1,4,256,256]{5,4,3,2,1,0:T(8,128)}, f32[2,3,1,4,256,256]{5,4,3,2,1,0:T(8,128)}) fusion(f32[2,3,2,4,256,256]{5,4,3,2,1,0:T(8,128)} %fusion.19), kind=kLoop, calls=%fused_computation.74 | loop fusion | flops 3145728 | bytes 25165824 | tf_op jit(solution)/shard_map/mul | solution.py:56
  485.7 24.1 %maximum_add_fusion = f32[2,3,2,4,256,256]{5,4,3,2,1,0:T(8,128)} fusion(f32[2,3,1,4,256,256]{5,4,3,2,1,0:T(8,128)} %get-tuple-element.6, f32[2,3,1,4,256,256]{5,4,3,2,1,0:T(8,128)} %get-tuple-element.5, f32[2,3,2,4,256,256]{5,4,3,2,1,0:T(8,128)} %copy-done.4, f32[2,3,1,4,256,256]{5,4,3,2,1,0:T(8,128)} %get-tuple-element.10, ...), kind=kLoop, calls=%fused_computation.69 | loop fusion | flops 25165824 | bytes 75497472 | tf_op jit(solution)/shard_map/add | solution.py:98
  509.8 6.0 fusion.33
  515.8 2.1 fusion.52
  517.9 2.1 convolution_bitcast_fusion.1
  520.0 1.7 copy.18
  521.6 10.5 %all-to-all-start = ((f32[4,256,256]{2,0,1:T(4,128)}), f32[4,256,256]{2,0,1:T(4,128)S(1)}, u32[]{:S(2)}, u32[]{:S(2)}) async-start(f32[4,256,256]{2,0,1:T(4,128)} %copy.18), calls=%async_computation | async-start | bytes 2097152 | tf_op jit(solution)/shard_map/all_to_all | solution.py:70
  532.4 13.6 %all-to-all-done = f32[4,256,256]{2,0,1:T(4,128)S(1)} async-done(((f32[4,256,256]{2,0,1:T(4,128)}), f32[4,256,256]{2,0,1:T(4,128)S(1)}, u32[]{:S(2)}, u32[]{:S(2)}) %all-to-all-start) | async-done | bytes 1048608 | tf_op jit(solution)/shard_map/all_to_all | solution.py:70
  546.4 1.8 convolution_multiply_fusion
  548.1 1.2 fusion.88
  549.9 17.7 %all_to_all.36 = f32[32,32,256]{2,1,0:T(8,128)S(1)} all-to-all(f32[32,32,256]{2,1,0:T(8,128)S(1)} %copy.22), channel_id=1, replica_groups=mesh['grp'=4,'grid'=8] {'grid'}, dimensions={0} | all-to-all | bytes 2097152 | tf_op jit(solution)/shard_map/all_to_all | solution.py:83
  567.8 2.1 convolution_bitcast_fusion
  569.9 2.1 fusion.50
  571.9 1.3 collective-permute-start.8
  573.3 18.2 %copy.32 = bf16[4,8,1024,256]{3,1,2,0:T(8,128)(2,1)} copy(bf16[4,8,1024,256]{3,2,1,0:T(8,128)(2,1)} %bitcast.51) | data formatting | bytes 33554432
  592.7 28.7 %collective-permute-done.8 = f32[4,256,256]{2,1,0:T(8,128)S(1)} collective-permute-done((f32[4,256,256]{2,1,0:T(8,128)S(1)}, f32[4,256,256]{2,1,0:T(8,128)S(1)}, u32[]{:S(2)}, u32[]{:S(2)}) %collective-permute-start.8) | collective-permute-done | bytes 1048608 | tf_op jit(solution)/shard_map/ppermute | solution.py:27
  621.6 3.5 multiply_convert_fusion
  625.0 5.2 convert_element_type.54
  630.2 11.5 %convolution_bitcast_fusion.2 = f32[32,6]{0,1:T(8,128)S(1)} fusion(bf16[6,262144]{1,0:T(8,128)(2,1)} %convert_element_type.54, bf16[32,262144]{1,0:T(8,128)(2,1)} %bitcast.50), kind=kOutput, calls=%fused_computation.92 | convolution fusion | flops 100663296 | bytes 19923712 | tf_op jit(solution)/shard_map/dot_general | solution.py:106
  641.7 13.5 %all-reduce.8 = f32[32,6]{0,1:T(8,128)S(1)} all-reduce(f32[32,6]{0,1:T(8,128)S(1)} %convolution_bitcast_fusion.2), channel_id=2, replica_groups=mesh['grp'=4,'grid'=8] {'grid'}, use_global_device_ids=true, to_apply=%region_1.2.clone | all-reduce | flops 192 | bytes 1536
  (42 shorter events, 6.8 us)
Async XLA Ops:
  0.0 4.6 copy-start.6
  4.6 10.9 %copy-start.7 = (f32[1,4,256,256]{3,2,1,0:T(8,128)S(1)}, f32[1,4,256,256]{3,2,1,0:T(8,128)}, u32[]{:S(2)}) copy-start(f32[1,4,256,256]{3,2,1,0:T(8,128)} %param.6) | copy-start | bytes 3145732
  4.6 10.9 %copy-start.9 = (f32[4,256,256]{2,1,0:T(8,128)S(1)}, f32[4,256,256]{2,1,0:T(8,128)}, u32[]{:S(2)}) copy-start(f32[4,256,256]{2,1,0:T(8,128)} %param.5) | copy-start | bytes 3145732
  5.7 4.5 copy-start.4
  10.8 69.3 %collective-permute-start = (f32[2,3,2,1,256,256]{5,4,3,2,1,0:T(8,128)S(1)}, f32[2,3,2,1,256,256]{5,4,3,2,1,0:T(8,128)}, u32[]{:S(2)}, u32[]{:S(2)}) collective-permute-start(f32[2,3,2,1,256,256]{5,4,3,2,1,0:T(8,128)S(1)} %get-tuple-element.19), channel_id=1, source_target_pairs={{1,0},{2,1},{3,2},{4,3},{5,4},{6,5},{7,6},{9,8},{10,9},{11,10},{12... | collective-permute-start | bytes 9437192 | tf_op jit(solution)/shard_map/ppermute | solution.py:19
  13.6 69.6 %collective-permute-start.1 = (f32[2,3,2,1,256,256]{5,4,3,2,1,0:T(8,128)S(1)}, f32[2,3,2,1,256,256]{5,4,3,2,1,0:T(8,128)}, u32[]{:S(2)}, u32[]{:S(2)}) collective-permute-start(f32[2,3,2,1,256,256]{5,4,3,2,1,0:T(8,128)S(1)} %get-tuple-element.20), channel_id=1, source_target_pairs={{0,1},{1,2},{2,3},{3,4},{4,5},{5,6},{6,7},{8,9},{9,10},{10,11},{11... | collective-permute-start | bytes 9437192 | tf_op jit(solution)/shard_map/ppermute | solution.py:16
  15.9 67.3 %copy-start.5 = (f32[2,4,256,256]{3,2,1,0:T(8,128)}, f32[2,4,256,256]{3,2,1,0:T(8,128)S(1)}, u32[]{:S(2)}) copy-start(f32[2,4,256,256]{3,2,1,0:T(8,128)S(1)} %pad_maximum_fusion.17) | copy-start | bytes 6291460
  125.1 20.4 %copy-start = (f32[2,3,1,4,256,256]{5,4,3,2,1,0:T(8,128)}, f32[2,3,1,4,256,256]{5,4,3,2,1,0:T(8,128)S(1)}, u32[]{:S(2)}) copy-start(f32[2,3,1,4,256,256]{5,4,3,2,1,0:T(8,128)S(1)} %get-tuple-element.17) | copy-start | bytes 18874372
  132.5 67.9 %collective-permute-start.2 = (f32[2,3,2,1,256,256]{5,4,3,2,1,0:T(8,128)}, f32[2,3,2,1,256,256]{5,4,3,2,1,0:T(8,128)}, u32[]{:S(2)}, u32[]{:S(2)}) collective-permute-start(f32[2,3,2,1,256,256]{5,4,3,2,1,0:T(8,128)} %get-tuple-element.15), channel_id=1, source_target_pairs={{1,0},{2,1},{3,2},{4,3},{5,4},{6,5},{7,6},{9,8},{10,9},{11,10},{12... | collective-permute-start | bytes 9437192 | tf_op jit(solution)/shard_map/ppermute | solution.py:19
  134.4 67.0 %collective-permute-start.3 = (f32[2,3,2,1,256,256]{5,4,3,2,1,0:T(8,128)}, f32[2,3,2,1,256,256]{5,4,3,2,1,0:T(8,128)}, u32[]{:S(2)}, u32[]{:S(2)}) collective-permute-start(f32[2,3,2,1,256,256]{5,4,3,2,1,0:T(8,128)} %get-tuple-element.16), channel_id=1, source_target_pairs={{0,1},{1,2},{2,3},{3,4},{4,5},{5,6},{6,7},{8,9},{9,10},{10,11},{11... | collective-permute-start | bytes 9437192 | tf_op jit(solution)/shard_map/ppermute | solution.py:16
  244.6 22.2 %copy-start.1 = (f32[2,3,1,4,256,256]{5,4,3,2,1,0:T(8,128)}, f32[2,3,1,4,256,256]{5,4,3,2,1,0:T(8,128)S(1)}, u32[]{:S(2)}) copy-start(f32[2,3,1,4,256,256]{5,4,3,2,1,0:T(8,128)S(1)} %get-tuple-element.13) | copy-start | bytes 18874372
  252.1 68.7 %collective-permute-start.4 = (f32[2,3,2,1,256,256]{5,4,3,2,1,0:T(8,128)}, f32[2,3,2,1,256,256]{5,4,3,2,1,0:T(8,128)}, u32[]{:S(2)}, u32[]{:S(2)}) collective-permute-start(f32[2,3,2,1,256,256]{5,4,3,2,1,0:T(8,128)} %get-tuple-element.11), channel_id=1, source_target_pairs={{1,0},{2,1},{3,2},{4,3},{5,4},{6,5},{7,6},{9,8},{10,9},{11,10},{12... | collective-permute-start | bytes 9437192 | tf_op jit(solution)/shard_map/ppermute | solution.py:19
  255.8 65.0 %collective-permute-start.5 = (f32[2,3,2,1,256,256]{5,4,3,2,1,0:T(8,128)}, f32[2,3,2,1,256,256]{5,4,3,2,1,0:T(8,128)}, u32[]{:S(2)}, u32[]{:S(2)}) collective-permute-start(f32[2,3,2,1,256,256]{5,4,3,2,1,0:T(8,128)} %get-tuple-element.12), channel_id=1, source_target_pairs={{0,1},{1,2},{2,3},{3,4},{4,5},{5,6},{6,7},{8,9},{9,10},{10,11},{11... | collective-permute-start | bytes 9437192 | tf_op jit(solution)/shard_map/ppermute | solution.py:16
  363.9 24.0 %copy-start.2 = (f32[2,3,1,4,256,256]{5,4,3,2,1,0:T(8,128)}, f32[2,3,1,4,256,256]{5,4,3,2,1,0:T(8,128)S(1)}, u32[]{:S(2)}) copy-start(f32[2,3,1,4,256,256]{5,4,3,2,1,0:T(8,128)S(1)} %get-tuple-element.9) | copy-start | bytes 18874372
  371.3 68.6 %collective-permute-start.6 = (f32[2,3,2,1,256,256]{5,4,3,2,1,0:T(8,128)}, f32[2,3,2,1,256,256]{5,4,3,2,1,0:T(8,128)}, u32[]{:S(2)}, u32[]{:S(2)}) collective-permute-start(f32[2,3,2,1,256,256]{5,4,3,2,1,0:T(8,128)} %get-tuple-element.7), channel_id=1, source_target_pairs={{1,0},{2,1},{3,2},{4,3},{5,4},{6,5},{7,6},{9,8},{10,9},{11,10},{12... | collective-permute-start | bytes 9437192 | tf_op jit(solution)/shard_map/ppermute | solution.py:19
  376.1 63.9 %collective-permute-start.7 = (f32[2,3,2,1,256,256]{5,4,3,2,1,0:T(8,128)}, f32[2,3,2,1,256,256]{5,4,3,2,1,0:T(8,128)}, u32[]{:S(2)}, u32[]{:S(2)}) collective-permute-start(f32[2,3,2,1,256,256]{5,4,3,2,1,0:T(8,128)} %get-tuple-element.8), channel_id=1, source_target_pairs={{0,1},{1,2},{2,3},{3,4},{4,5},{5,6},{6,7},{8,9},{9,10},{10,11},{11... | collective-permute-start | bytes 9437192 | tf_op jit(solution)/shard_map/ppermute | solution.py:16
  474.5 11.2 %copy-start.3 = (f32[2,3,1,4,256,256]{5,4,3,2,1,0:T(8,128)S(1)}, f32[2,3,1,4,256,256]{5,4,3,2,1,0:T(8,128)}, u32[]{:S(2)}) copy-start(f32[2,3,1,4,256,256]{5,4,3,2,1,0:T(8,128)} %copy-done.2) | copy-start | bytes 18874372
  521.6 24.4 %all-to-all-start = ((f32[4,256,256]{2,0,1:T(4,128)}), f32[4,256,256]{2,0,1:T(4,128)S(1)}, u32[]{:S(2)}, u32[]{:S(2)}) async-start(f32[4,256,256]{2,0,1:T(4,128)} %copy.18), calls=%async_computation | async-start | bytes 2097152 | tf_op jit(solution)/shard_map/all_to_all | solution.py:70
  571.9 49.5 %collective-permute-start.8 = (f32[4,256,256]{2,1,0:T(8,128)S(1)}, f32[4,256,256]{2,1,0:T(8,128)S(1)}, u32[]{:S(2)}, u32[]{:S(2)}) collective-permute-start(f32[4,256,256]{2,1,0:T(8,128)S(1)} %fusion.50), channel_id=1, source_target_pairs={{0,16},{8,24},{1,17},{9,25},{2,18},{10,26},{3,19},{11,27},{4,20},{... | collective-permute-start | bytes 3145736 | tf_op jit(solution)/shard_map/ppermute | solution.py:27
  573.3 18.2 %copy-start.10 = (u32[32]{0:T(128)S(1)}, u32[32]{0:T(128)}, u32[]{:S(2)}) copy-start(u32[32]{0:T(128)} %constant.111) | copy-start | bytes 388
  573.3 48.2 %copy-start.8 = (f32[1,4,256,256]{3,2,1,0:T(8,128)S(1)}, f32[1,4,256,256]{3,2,1,0:T(8,128)}, u32[]{:S(2)}) copy-start(f32[1,4,256,256]{3,2,1,0:T(8,128)} %param.6) | copy-start | bytes 3145732
where the time goes:
time: 665 us; the launch traced here: 656 us
  waiting for transfers between devices  271 us (41%)
  other arithmetic  257 us (39%)
  local copies, waits for them, and re-layouts  38.3 us (6%)
  starting transfers between devices  34.5 us (5%)
  blocking collectives  31.2 us (5%)
  matrix products  22.7 us (3%)
    ppermute x4, waiting for transfers between devices, padded_2(): lax.ppermute(lax.slice_in_dim(block, 0, width, axis=dim), axis, backward)  225 us
    add x4, other arithmetic, on_device(): applied = -0.5 * laplace_inner(padded) + fields[:, None, None] * current  137 us
    another operation x6, other arithmetic, taylor_term(): jnp.stack([factor * applied[:, :, 1], -factor * applied[:, :, 0]], axis=2)  48.5 us
    mul x4, other arithmetic, taylor_term(): factor * applied[:, :, 1]  37.4 us
    ppermute x1, waiting for transfers between devices, shifted(): return lax.ppermute(array, axis, pairs)  28.7 us
    unnamed x26, local copies, waits for them, and re-layouts  28 us
    add x1, other arithmetic, on_device(): summed = summed + current  24.1 us
    all_to_all x1, blocking collectives, poisson_block(): lax.all_to_all(field, 'grid', split_axis=0, concat_axis=1, tiled=True)  17.7 us
  transfers between devices with their start and end apart: 10, of which 8 were waited for; matrix products, arithmetic and copies ran while one was open for 7% of the time, Pallas kernels for 0%

commit v1 on v0

--- a/solution.py
+++ b/solution.py
@@ -6,6 +6,18 @@
 ORDER = 4
 time_step = 0.2
 four_pi = 12.566370614359172
+
+
+def roots_run(local_x):
+    return jnp.concatenate(
+        lax.all_to_all(
+            jnp.stack(jnp.split(local_x, lax.axis_size("grid"), 1), axis=0),
+            axis_name="grid",
+            split_axis=0,
+            concat_axis=0,
+        ),
+        0,
+    )
 
 
 def padded_2(block, sides, width):
@@ -67,7 +79,7 @@
     table_z = sine_table(size_z)
     field = jnp.einsum("xyz,zl->xyl", density, table_z, precision=highest)
     field = jnp.einsum("xyl,yk->xkl", field, table_y, precision=highest)
-    columns = lax.all_to_all(field, "grid", split_axis=1, concat_axis=0, tiled=True)
+    columns = roots_run(field)
     row_count = columns.shape[1]
     own_rows = lax.dynamic_slice_in_dim(
         eigenvalues(size_y), lax.axis_index("grid") * row_count, row_count

time: 665 us -> 668 us (level)
    unnamed x26 -> x33, local copies, waits for them, and re-layouts: 28 us -> 32.6 us
where the time goes in v1:
time: 668 us; the launch traced here: 660 us
  waiting for transfers between devices  272 us (41%)
  other arithmetic  257 us (38%)
  local copies, waits for them, and re-layouts  41.6 us (6%)
  starting transfers between devices  34.3 us (5%)
  blocking collectives  31.2 us (5%)
  matrix products  22.7 us (3%)
    ppermute x4, waiting for transfers between devices, padded_2(): lax.ppermute(lax.slice_in_dim(block, 0, width, axis=dim), axis, backward)  225 us
    add x4, other arithmetic, on_device(): applied = -0.5 * laplace_inner(padded) + fields[:, None, None] * current  137 us
    another operation x6, other arithmetic, taylor_term(): jnp.stack([factor * applied[:, :, 1], -factor * applied[:, :, 0]], axis=2)  48.4 us
    mul x4, other arithmetic, taylor_term(): factor * applied[:, :, 1]  37.5 us
    unnamed x33, local copies, waits for them, and re-layouts  32.6 us
    ppermute x1, waiting for transfers between devices, shifted(): return lax.ppermute(array, axis, pairs)  28.7 us
    add x1, other arithmetic, on_device(): summed = summed + current  24.1 us
    all_to_all x1, blocking collectives, poisson_block(): lax.all_to_all(field, 'grid', split_axis=0, concat_axis=1, tiled=True)  17.7 us
  transfers between devices with their start and end apart: 10, of which 8 were waited for; matrix products, arithmetic and copies ran while one was open for 7% of the time, Pallas kernels for 0%

profile of v1, /device:TPU:28, one launch (start us, length us, event | category | flops | bytes accessed | tf_op | source)
XLA Modules:
  0.0 659.6 jit_solution(8340969548988594998)
XLA Ops:
  0.0 3.6 constant_dynamic-update-slice_fusion.1
  4.6 1.1 constant_dynamic-update-slice_fusion
  5.7 4.5 copy-done.4
  10.8 2.8 collective-permute-start
  13.6 1.9 collective-permute-start.1
  15.9 64.2 %collective-permute-done = f32[2,3,2,1,256,256]{5,4,3,2,1,0:T(8,128)} collective-permute-done((f32[2,3,2,1,256,256]{5,4,3,2,1,0:T(8,128)S(1)}, f32[2,3,2,1,256,256]{5,4,3,2,1,0:T(8,128)}, u32[]{:S(2)}, u32[]{:S(2)}) %collective-permute-start) | collective-permute-done | bytes 3145760 | tf_op jit(solution)/shard_map/ppermute | solution.py:31
  80.1 3.1 collective-permute-done.1
  83.2 33.2 %fusion.4 = f32[2,3,2,4,256,256]{5,4,3,2,1,0:T(8,128)} fusion(f32[2,3,2,4,256,256]{5,4,3,2,1,0:T(8,128)} %copy-done.4, f32[2,3,2,1,256,256]{5,4,3,2,1,0:T(8,128)} %collective-permute-done.1, f32[2,3,2,1,256,256]{5,4,3,2,1,0:T(8,128)} %collective-permute-done, f32[2,4,256,256]{3,2,1,0:T(8,128)S(1)} %pad_maximum_fusion.17), kind=kLoop, calls=%fused_computation.27 | loop fusion | flops 37748736 | bytes 33554432 | tf_op jit(solution)/shard_map/add | solution.py:108
  116.4 8.8 %slice_multiply_fusion.8 = (f32[2,3,1,4,256,256]{5,4,3,2,1,0:T(8,128)S(1)}, f32[2,3,1,4,256,256]{5,4,3,2,1,0:T(8,128)}) fusion(f32[2,3,2,4,256,256]{5,4,3,2,1,0:T(8,128)} %fusion.4), kind=kLoop, calls=%fused_computation.80 | loop fusion | flops 3145728 | bytes 25165824 | tf_op jit(solution)/shard_map/mul | solution.py:68
  125.1 7.3 %fusion.38 = (f32[2,3,2,1,256,256]{5,4,3,2,1,0:T(8,128)}, f32[2,3,2,1,256,256]{5,4,3,2,1,0:T(8,128)}) fusion(f32[2,3,1,4,256,256]{5,4,3,2,1,0:T(8,128)S(1)} %get-tuple-element.17, f32[2,3,1,4,256,256]{5,4,3,2,1,0:T(8,128)} %get-tuple-element.18), kind=kLoop, calls=%fused_computation.86 | loop fusion | flops 1572864 | bytes 18874368 | tf_op jit(solution)/shard_map/stack | solution.py:68
  132.5 1.9 collective-permute-start.2
  134.4 2.4 collective-permute-start.3
  136.8 8.7 %pad_maximum_fusion = f32[2,3,2,4,256,256]{5,4,3,2,1,0:T(8,128)} fusion(f32[2,3,1,4,256,256]{5,4,3,2,1,0:T(8,128)} %get-tuple-element.18, f32[2,3,1,4,256,256]{5,4,3,2,1,0:T(8,128)S(1)} %get-tuple-element.17), kind=kLoop, calls=%fused_computation.10 | loop fusion | flops 3145728 | bytes 25165824 | tf_op jit(solution)/shard_map/stack | solution.py:68
  145.5 54.8 %collective-permute-done.2 = f32[2,3,2,1,256,256]{5,4,3,2,1,0:T(8,128)} collective-permute-done((f32[2,3,2,1,256,256]{5,4,3,2,1,0:T(8,128)}, f32[2,3,2,1,256,256]{5,4,3,2,1,0:T(8,128)}, u32[]{:S(2)}, u32[]{:S(2)}) %collective-permute-start.2) | collective-permute-done | bytes 3145760 | tf_op jit(solution)/shard_map/ppermute | solution.py:31
  201.4 34.5 %fusion.9 = f32[2,3,2,4,256,256]{5,4,3,2,1,0:T(8,128)} fusion(f32[2,3,2,4,256,256]{5,4,3,2,1,0:T(8,128)} %pad_maximum_fusion, f32[2,3,2,1,256,256]{5,4,3,2,1,0:T(8,128)} %collective-permute-done.3, f32[2,3,1,4,256,256]{5,4,3,2,1,0:T(8,128)} %get-tuple-element.18, f32[2,3,1,4,256,256]{5,4,3,2,1,0:T(8,128)} %copy-done, ...), kind=kLoop, calls=%fused_computation.32 | loop fusion | flops 44040192 | bytes 46137344 | tf_op jit(solution)/shard_map/add | solution.py:108
  235.8 8.8 %slice_multiply_fusion.6 = (f32[2,3,1,4,256,256]{5,4,3,2,1,0:T(8,128)S(1)}, f32[2,3,1,4,256,256]{5,4,3,2,1,0:T(8,128)}) fusion(f32[2,3,2,4,256,256]{5,4,3,2,1,0:T(8,128)} %fusion.9), kind=kLoop, calls=%fused_computation.78 | loop fusion | flops 3145728 | bytes 25165824 | tf_op jit(solution)/shard_map/mul | solution.py:68
  244.6 7.5 %fusion.36 = (f32[2,3,2,1,256,256]{5,4,3,2,1,0:T(8,128)}, f32[2,3,2,1,256,256]{5,4,3,2,1,0:T(8,128)}) fusion(f32[2,3,1,4,256,256]{5,4,3,2,1,0:T(8,128)S(1)} %get-tuple-element.13, f32[2,3,1,4,256,256]{5,4,3,2,1,0:T(8,128)} %get-tuple-element.14), kind=kLoop, calls=%fused_computation.84 | loop fusion | flops 1572864 | bytes 18874368 | tf_op jit(solution)/shard_map/stack | solution.py:68
  252.1 3.7 collective-permute-start.4
  255.8 2.2 collective-permute-start.5
  258.0 8.8 %pad_maximum_fusion.1 = f32[2,3,2,4,256,256]{5,4,3,2,1,0:T(8,128)} fusion(f32[2,3,1,4,256,256]{5,4,3,2,1,0:T(8,128)} %get-tuple-element.14, f32[2,3,1,4,256,256]{5,4,3,2,1,0:T(8,128)S(1)} %get-tuple-element.13), kind=kLoop, calls=%fused_computation.15 | loop fusion | flops 3145728 | bytes 25165824 | tf_op jit(solution)/shard_map/stack | solution.py:68
  266.8 54.0 %collective-permute-done.4 = f32[2,3,2,1,256,256]{5,4,3,2,1,0:T(8,128)} collective-permute-done((f32[2,3,2,1,256,256]{5,4,3,2,1,0:T(8,128)}, f32[2,3,2,1,256,256]{5,4,3,2,1,0:T(8,128)}, u32[]{:S(2)}, u32[]{:S(2)}) %collective-permute-start.4) | collective-permute-done | bytes 3145760 | tf_op jit(solution)/shard_map/ppermute | solution.py:31
  320.8 34.4 %fusion.14 = f32[2,3,2,4,256,256]{5,4,3,2,1,0:T(8,128)} fusion(f32[2,3,2,4,256,256]{5,4,3,2,1,0:T(8,128)} %pad_maximum_fusion.1, f32[2,3,2,1,256,256]{5,4,3,2,1,0:T(8,128)} %collective-permute-done.5, f32[2,3,1,4,256,256]{5,4,3,2,1,0:T(8,128)} %get-tuple-element.14, f32[2,3,1,4,256,256]{5,4,3,2,1,0:T(8,128)} %copy-done.1, ...), kind=kLoop, calls=%fused_computation.37 | loop fusion | flops 44040192 | bytes 46137344 | tf_op jit(solution)/shard_map/add | solution.py:108
  355.2 8.8 %slice_multiply_fusion.4 = (f32[2,3,1,4,256,256]{5,4,3,2,1,0:T(8,128)S(1)}, f32[2,3,1,4,256,256]{5,4,3,2,1,0:T(8,128)}) fusion(f32[2,3,2,4,256,256]{5,4,3,2,1,0:T(8,128)} %fusion.14), kind=kLoop, calls=%fused_computation.76 | loop fusion | flops 3145728 | bytes 25165824 | tf_op jit(solution)/shard_map/mul | solution.py:68
  364.0 7.4 %fusion.34 = (f32[2,3,2,1,256,256]{5,4,3,2,1,0:T(8,128)}, f32[2,3,2,1,256,256]{5,4,3,2,1,0:T(8,128)}) fusion(f32[2,3,1,4,256,256]{5,4,3,2,1,0:T(8,128)S(1)} %get-tuple-element.9, f32[2,3,1,4,256,256]{5,4,3,2,1,0:T(8,128)} %get-tuple-element.10), kind=kLoop, calls=%fused_computation.82 | loop fusion | flops 1572864 | bytes 18874368 | tf_op jit(solution)/shard_map/stack | solution.py:68
  371.4 4.7 collective-permute-start.6
  376.1 3.1 collective-permute-start.7
  379.2 8.7 %pad_maximum_fusion.2 = f32[2,3,2,4,256,256]{5,4,3,2,1,0:T(8,128)} fusion(f32[2,3,1,4,256,256]{5,4,3,2,1,0:T(8,128)} %get-tuple-element.10, f32[2,3,1,4,256,256]{5,4,3,2,1,0:T(8,128)S(1)} %get-tuple-element.9), kind=kLoop, calls=%fused_computation.20 | loop fusion | flops 3145728 | bytes 25165824 | tf_op jit(solution)/shard_map/stack | solution.py:68
  387.9 52.2 %collective-permute-done.6 = f32[2,3,2,1,256,256]{5,4,3,2,1,0:T(8,128)} collective-permute-done((f32[2,3,2,1,256,256]{5,4,3,2,1,0:T(8,128)}, f32[2,3,2,1,256,256]{5,4,3,2,1,0:T(8,128)}, u32[]{:S(2)}, u32[]{:S(2)}) %collective-permute-start.6) | collective-permute-done | bytes 3145760 | tf_op jit(solution)/shard_map/ppermute | solution.py:31
  440.0 34.5 %fusion.19 = f32[2,3,2,4,256,256]{5,4,3,2,1,0:T(8,128)} fusion(f32[2,3,2,4,256,256]{5,4,3,2,1,0:T(8,128)} %pad_maximum_fusion.2, f32[2,3,2,1,256,256]{5,4,3,2,1,0:T(8,128)} %collective-permute-done.7, f32[2,3,1,4,256,256]{5,4,3,2,1,0:T(8,128)} %get-tuple-element.10, f32[2,3,1,4,256,256]{5,4,3,2,1,0:T(8,128)} %copy-done.2, ...), kind=kLoop, calls=%fused_computation.42 | loop fusion | flops 44040192 | bytes 46137344 | tf_op jit(solution)/shard_map/add | solution.py:108
  474.6 11.2 %slice_multiply_fusion.2 = (f32[2,3,1,4,256,256]{5,4,3,2,1,0:T(8,128)}, f32[2,3,1,4,256,256]{5,4,3,2,1,0:T(8,128)}) fusion(f32[2,3,2,4,256,256]{5,4,3,2,1,0:T(8,128)} %fusion.19), kind=kLoop, calls=%fused_computation.74 | loop fusion | flops 3145728 | bytes 25165824 | tf_op jit(solution)/shard_map/mul | solution.py:68
  485.7 24.1 %maximum_add_fusion = f32[2,3,2,4,256,256]{5,4,3,2,1,0:T(8,128)} fusion(f32[2,3,1,4,256,256]{5,4,3,2,1,0:T(8,128)} %get-tuple-element.6, f32[2,3,1,4,256,256]{5,4,3,2,1,0:T(8,128)} %get-tuple-element.5, f32[2,3,2,4,256,256]{5,4,3,2,1,0:T(8,128)} %copy-done.4, f32[2,3,1,4,256,256]{5,4,3,2,1,0:T(8,128)} %get-tuple-element.10, ...), kind=kLoop, calls=%fused_computation.69 | loop fusion | flops 25165824 | bytes 75497472 | tf_op jit(solution)/shard_map/add | solution.py:110
  509.8 6.0 fusion.33
  515.8 2.1 fusion.52
  517.9 2.1 convolution_bitcast_fusion.1
  525.3 10.3 %all-to-all-start = ((f32[8,4,32,256]{3,2,1,0:T(8,128)}), f32[8,4,32,256]{3,2,1,0:T(8,128)S(1)}, u32[]{:S(2)}, u32[]{:S(2)}) async-start(f32[8,4,32,256]{3,2,1,0:T(8,128)} %fusion.56), calls=%async_computation | async-start | bytes 2097152 | tf_op jit(solution)/shard_map/all_to_all | solution.py:13
  535.9 13.6 %all-to-all-done = f32[8,4,32,256]{3,2,1,0:T(8,128)S(1)} async-done(((f32[8,4,32,256]{3,2,1,0:T(8,128)}), f32[8,4,32,256]{3,2,1,0:T(8,128)S(1)}, u32[]{:S(2)}, u32[]{:S(2)}) %all-to-all-start) | async-done | bytes 1048608 | tf_op jit(solution)/shard_map/all_to_all | solution.py:13
  549.5 1.8 convolution_multiply_fusion
  551.3 1.2 fusion.96
  553.1 17.7 %all_to_all.23 = f32[32,32,256]{2,1,0:T(8,128)S(1)} all-to-all(f32[32,32,256]{2,1,0:T(8,128)S(1)} %copy.17), channel_id=1, replica_groups=mesh['grp'=4,'grid'=8] {'grid'}, dimensions={0} | all-to-all | bytes 2097152 | tf_op jit(solution)/shard_map/all_to_all | solution.py:95
  570.9 2.1 convolution_bitcast_fusion
  573.1 2.1 fusion.50
  575.1 1.3 collective-permute-start.8
  576.5 18.2 %copy.27 = bf16[4,8,1024,256]{3,1,2,0:T(8,128)(2,1)} copy(bf16[4,8,1024,256]{3,2,1,0:T(8,128)(2,1)} %bitcast.80) | data formatting | bytes 33554432
  595.9 28.7 %collective-permute-done.8 = f32[4,256,256]{2,1,0:T(8,128)S(1)} collective-permute-done((f32[4,256,256]{2,1,0:T(8,128)S(1)}, f32[4,256,256]{2,1,0:T(8,128)S(1)}, u32[]{:S(2)}, u32[]{:S(2)}) %collective-permute-start.8) | collective-permute-done | bytes 1048608 | tf_op jit(solution)/shard_map/ppermute | solution.py:39
  624.8 3.5 multiply_convert_fusion
  628.2 5.2 convert_element_type.54
  633.4 11.5 %convolution_bitcast_fusion.2 = f32[32,6]{0,1:T(8,128)S(1)} fusion(bf16[6,262144]{1,0:T(8,128)(2,1)} %convert_element_type.54, bf16[32,262144]{1,0:T(8,128)(2,1)} %bitcast.79), kind=kOutput, calls=%fused_computation.92 | convolution fusion | flops 100663296 | bytes 19923712 | tf_op jit(solution)/shard_map/dot_general | solution.py:118
  644.9 13.5 %all-reduce.8 = f32[32,6]{0,1:T(8,128)S(1)} all-reduce(f32[32,6]{0,1:T(8,128)S(1)} %convolution_bitcast_fusion.2), channel_id=2, replica_groups=mesh['grp'=4,'grid'=8] {'grid'}, use_global_device_ids=true, to_apply=%region_1.2.clone | all-reduce | flops 192 | bytes 1536
  (47 shorter events, 10.7 us)
Async XLA Ops:
  0.0 4.6 copy-start.6
  4.6 10.9 %copy-start.7 = (f32[1,4,256,256]{3,2,1,0:T(8,128)S(1)}, f32[1,4,256,256]{3,2,1,0:T(8,128)}, u32[]{:S(2)}) copy-start(f32[1,4,256,256]{3,2,1,0:T(8,128)} %param.6) | copy-start | bytes 3145732
  4.6 10.9 %copy-start.9 = (f32[4,256,256]{2,1,0:T(8,128)S(1)}, f32[4,256,256]{2,1,0:T(8,128)}, u32[]{:S(2)}) copy-start(f32[4,256,256]{2,1,0:T(8,128)} %param.5) | copy-start | bytes 3145732
  5.7 4.5 copy-start.4
  10.8 69.3 %collective-permute-start = (f32[2,3,2,1,256,256]{5,4,3,2,1,0:T(8,128)S(1)}, f32[2,3,2,1,256,256]{5,4,3,2,1,0:T(8,128)}, u32[]{:S(2)}, u32[]{:S(2)}) collective-permute-start(f32[2,3,2,1,256,256]{5,4,3,2,1,0:T(8,128)S(1)} %get-tuple-element.19), channel_id=1, source_target_pairs={{1,0},{2,1},{3,2},{4,3},{5,4},{6,5},{7,6},{9,8},{10,9},{11,10},{12... | collective-permute-start | bytes 9437192 | tf_op jit(solution)/shard_map/ppermute | solution.py:31
  13.6 69.6 %collective-permute-start.1 = (f32[2,3,2,1,256,256]{5,4,3,2,1,0:T(8,128)S(1)}, f32[2,3,2,1,256,256]{5,4,3,2,1,0:T(8,128)}, u32[]{:S(2)}, u32[]{:S(2)}) collective-permute-start(f32[2,3,2,1,256,256]{5,4,3,2,1,0:T(8,128)S(1)} %get-tuple-element.20), channel_id=1, source_target_pairs={{0,1},{1,2},{2,3},{3,4},{4,5},{5,6},{6,7},{8,9},{9,10},{10,11},{11... | collective-permute-start | bytes 9437192 | tf_op jit(solution)/shard_map/ppermute | solution.py:28
  15.9 67.3 %copy-start.5 = (f32[2,4,256,256]{3,2,1,0:T(8,128)}, f32[2,4,256,256]{3,2,1,0:T(8,128)S(1)}, u32[]{:S(2)}) copy-start(f32[2,4,256,256]{3,2,1,0:T(8,128)S(1)} %pad_maximum_fusion.17) | copy-start | bytes 6291460
  125.1 20.4 %copy-start = (f32[2,3,1,4,256,256]{5,4,3,2,1,0:T(8,128)}, f32[2,3,1,4,256,256]{5,4,3,2,1,0:T(8,128)S(1)}, u32[]{:S(2)}) copy-start(f32[2,3,1,4,256,256]{5,4,3,2,1,0:T(8,128)S(1)} %get-tuple-element.17) | copy-start | bytes 18874372
  132.5 67.9 %collective-permute-start.2 = (f32[2,3,2,1,256,256]{5,4,3,2,1,0:T(8,128)}, f32[2,3,2,1,256,256]{5,4,3,2,1,0:T(8,128)}, u32[]{:S(2)}, u32[]{:S(2)}) collective-permute-start(f32[2,3,2,1,256,256]{5,4,3,2,1,0:T(8,128)} %get-tuple-element.15), channel_id=1, source_target_pairs={{1,0},{2,1},{3,2},{4,3},{5,4},{6,5},{7,6},{9,8},{10,9},{11,10},{12... | collective-permute-start | bytes 9437192 | tf_op jit(solution)/shard_map/ppermute | solution.py:31
  134.4 67.0 %collective-permute-start.3 = (f32[2,3,2,1,256,256]{5,4,3,2,1,0:T(8,128)}, f32[2,3,2,1,256,256]{5,4,3,2,1,0:T(8,128)}, u32[]{:S(2)}, u32[]{:S(2)}) collective-permute-start(f32[2,3,2,1,256,256]{5,4,3,2,1,0:T(8,128)} %get-tuple-element.16), channel_id=1, source_target_pairs={{0,1},{1,2},{2,3},{3,4},{4,5},{5,6},{6,7},{8,9},{9,10},{10,11},{11... | collective-permute-start | bytes 9437192 | tf_op jit(solution)/shard_map/ppermute | solution.py:28
  244.6 22.2 %copy-start.1 = (f32[2,3,1,4,256,256]{5,4,3,2,1,0:T(8,128)}, f32[2,3,1,4,256,256]{5,4,3,2,1,0:T(8,128)S(1)}, u32[]{:S(2)}) copy-start(f32[2,3,1,4,256,256]{5,4,3,2,1,0:T(8,128)S(1)} %get-tuple-element.13) | copy-start | bytes 18874372
  252.1 68.7 %collective-permute-start.4 = (f32[2,3,2,1,256,256]{5,4,3,2,1,0:T(8,128)}, f32[2,3,2,1,256,256]{5,4,3,2,1,0:T(8,128)}, u32[]{:S(2)}, u32[]{:S(2)}) collective-permute-start(f32[2,3,2,1,256,256]{5,4,3,2,1,0:T(8,128)} %get-tuple-element.11), channel_id=1, source_target_pairs={{1,0},{2,1},{3,2},{4,3},{5,4},{6,5},{7,6},{9,8},{10,9},{11,10},{12... | collective-permute-start | bytes 9437192 | tf_op jit(solution)/shard_map/ppermute | solution.py:31
  255.8 65.0 %collective-permute-start.5 = (f32[2,3,2,1,256,256]{5,4,3,2,1,0:T(8,128)}, f32[2,3,2,1,256,256]{5,4,3,2,1,0:T(8,128)}, u32[]{:S(2)}, u32[]{:S(2)}) collective-permute-start(f32[2,3,2,1,256,256]{5,4,3,2,1,0:T(8,128)} %get-tuple-element.12), channel_id=1, source_target_pairs={{0,1},{1,2},{2,3},{3,4},{4,5},{5,6},{6,7},{8,9},{9,10},{10,11},{11... | collective-permute-start | bytes 9437192 | tf_op jit(solution)/shard_map/ppermute | solution.py:28
  364.0 23.9 %copy-start.2 = (f32[2,3,1,4,256,256]{5,4,3,2,1,0:T(8,128)}, f32[2,3,1,4,256,256]{5,4,3,2,1,0:T(8,128)S(1)}, u32[]{:S(2)}) copy-start(f32[2,3,1,4,256,256]{5,4,3,2,1,0:T(8,128)S(1)} %get-tuple-element.9) | copy-start | bytes 18874372
  371.4 68.6 %collective-permute-start.6 = (f32[2,3,2,1,256,256]{5,4,3,2,1,0:T(8,128)}, f32[2,3,2,1,256,256]{5,4,3,2,1,0:T(8,128)}, u32[]{:S(2)}, u32[]{:S(2)}) collective-permute-start(f32[2,3,2,1,256,256]{5,4,3,2,1,0:T(8,128)} %get-tuple-element.7), channel_id=1, source_target_pairs={{1,0},{2,1},{3,2},{4,3},{5,4},{6,5},{7,6},{9,8},{10,9},{11,10},{12... | collective-permute-start | bytes 9437192 | tf_op jit(solution)/shard_map/ppermute | solution.py:31
  376.1 63.9 %collective-permute-start.7 = (f32[2,3,2,1,256,256]{5,4,3,2,1,0:T(8,128)}, f32[2,3,2,1,256,256]{5,4,3,2,1,0:T(8,128)}, u32[]{:S(2)}, u32[]{:S(2)}) collective-permute-start(f32[2,3,2,1,256,256]{5,4,3,2,1,0:T(8,128)} %get-tuple-element.8), channel_id=1, source_target_pairs={{0,1},{1,2},{2,3},{3,4},{4,5},{5,6},{6,7},{8,9},{9,10},{10,11},{11... | collective-permute-start | bytes 9437192 | tf_op jit(solution)/shard_map/ppermute | solution.py:28
  474.5 11.2 %copy-start.3 = (f32[2,3,1,4,256,256]{5,4,3,2,1,0:T(8,128)S(1)}, f32[2,3,1,4,256,256]{5,4,3,2,1,0:T(8,128)}, u32[]{:S(2)}) copy-start(f32[2,3,1,4,256,256]{5,4,3,2,1,0:T(8,128)} %copy-done.2) | copy-start | bytes 18874372
  525.3 24.2 %all-to-all-start = ((f32[8,4,32,256]{3,2,1,0:T(8,128)}), f32[8,4,32,256]{3,2,1,0:T(8,128)S(1)}, u32[]{:S(2)}, u32[]{:S(2)}) async-start(f32[8,4,32,256]{3,2,1,0:T(8,128)} %fusion.56), calls=%async_computation | async-start | bytes 2097152 | tf_op jit(solution)/shard_map/all_to_all | solution.py:13
  575.1 49.5 %collective-permute-start.8 = (f32[4,256,256]{2,1,0:T(8,128)S(1)}, f32[4,256,256]{2,1,0:T(8,128)S(1)}, u32[]{:S(2)}, u32[]{:S(2)}) collective-permute-start(f32[4,256,256]{2,1,0:T(8,128)S(1)} %fusion.50), channel_id=1, source_target_pairs={{0,16},{8,24},{1,17},{9,25},{2,18},{10,26},{3,19},{11,27},{4,20},{... | collective-permute-start | bytes 3145736 | tf_op jit(solution)/shard_map/ppermute | solution.py:39
  576.4 18.2 %copy-start.10 = (u32[32]{0:T(128)S(1)}, u32[32]{0:T(128)}, u32[]{:S(2)}) copy-start(u32[32]{0:T(128)} %constant.111) | copy-start | bytes 388
  576.4 48.2 %copy-start.8 = (f32[1,4,256,256]{3,2,1,0:T(8,128)S(1)}, f32[1,4,256,256]{3,2,1,0:T(8,128)}, u32[]{:S(2)}) copy-start(f32[1,4,256,256]{3,2,1,0:T(8,128)} %param.6) | copy-start | bytes 3145732
